TPU v7x, 32 devices: a whole 2x2x4 slice. The times are simulated.
32 devices in a mesh: groups: 1, ex: 16 (over z, y, core), layer: 2 (over x), pb: 1.
Axes of the slice: x: 2, y: 2, z: 4, core: 2. Of those that a mesh axis runs over, the one named last changes fastest.
Arguments:
- train_grads: float32 [2, 1536, 1024], P('layer', ('groups', 'ex')), may hold values from -64 to 64
- query_grads: float32 [2, 1, 512, 1024], P('layer', 'pb', ('groups', 'ex')), may hold values from -64 to 64
- damping: float32 [2], P('layer'), may hold values from 0.05 to 0.5
Outputs:
- influence: float32 [1536, 1, 512], P(('groups', 'ex'), 'pb', 'layer')
All inputs are finite; a program needn't handle non-finite values.
Results may differ from a plain program's by a relative error of at most 0.0003.
Values sent between devices are 32-bit elements; how exact they have to be, the bound alone decides.
A program may use at most 64 MiB of HBM per device.

v0:
```python
import jax
import jax.numpy as jnp
from jax import lax
from jax.sharding import PartitionSpec as P


def solve_rows(factor, rows_in):
    inner = lax.linalg.triangular_solve(
        factor, rows_in, left_side=False, lower=True, transpose_a=True
    )
    return lax.linalg.triangular_solve(
        factor, inner, left_side=False, lower=True, transpose_a=False
    )


def on_device(train_grads, query_grads, damping):
    layers_here, local_rows, coords = train_grads.shape
    total_rows = local_rows * lax.axis_size("ex")
    half_rows = local_rows // lax.axis_size("pb")
    own_rows = lax.dynamic_slice_in_dim(train_grads, lax.axis_index("pb") * half_rows, half_rows, 1)
    partial_gram = jnp.einsum("lnp,lnq->lpq", own_rows, own_rows, precision=lax.Precision.HIGHEST)
    gram_matrix = lax.psum(partial_gram, ("ex", "pb"))
    identity = jnp.eye(coords, dtype=jnp.float32)
    fisher = gram_matrix / total_rows + damping[:, None, None] * identity[None]
    factor = jnp.linalg.cholesky(fisher)
    queries = query_grads[:, 0]
    solved = solve_rows(factor, queries)
    score_tile = jnp.einsum(
        "lnp,lkp->nk",
        train_grads,
        lax.all_gather(solved, "ex", axis=1, tiled=True),
        precision=lax.Precision.HIGHEST,
    )
    shares = lax.psum_scatter(score_tile, "layer", scatter_dimension=1, tiled=True)
    return shares[:, None, :]


def solution(mesh):
    in_specs = (
        P("layer", ("groups", "ex"), None),
        P("layer", "pb", ("groups", "ex"), None),
        P("layer"),
    )
    out_specs = P(("groups", "ex"), "pb", "layer")
    return jax.shard_map(
        on_device, mesh=mesh, in_specs=in_specs, out_specs=out_specs, check_vma=False
    )
```

profile of v0, /device:TPU:0, one launch (start us, length us, event | category | flops | bytes accessed | tf_op | source)
XLA Modules:
  0.0 545.7 jit_solution(9678609055191033883)
XLA Ops:
  7.5 5.0 convolution_bitcast_fusion
  13.3 113.3 %all-reduce.3.cloned.1.call-done = f32[1,1024,1024]{1,2,0:T(8,128)} async-done(((f32[1,1024,1024]{1,2,0:T(8,128)}), f32[1,1024,1024]{1,2,0:T(8,128)}) %all-reduce.3.cloned.1.call-update) | async-done | bytes 4194320 | tf_op jit(solution)/shard_map/psum | solution.py:22
  126.6 5.1 select_add_fusion
  131.7 5.6 %copy.5 = f32[1,1024,1024]{2,1,0:T(8,128)} copy(f32[1,1024,1024]{1,2,0:T(8,128)} %select_add_fusion) | data formatting | bytes 8388608 | tf_op jit(solution)/shard_map/add | solution.py:24
  143.7 11.7 %custom-call.72 = f32[1,128,128]{2,1,0:T(8,128)S(1)} custom-call(f32[1,128,128]{2,1,0:T(8,128)S(1)} %cholesky.582), custom_call_target="Cholesky" | custom-call | tf_op jit(solution)/shard_map/jit(cholesky)/cholesky | solution.py:25
  155.6 9.8 %custom-call.73 = f32[1,1,128,128]{2,3,1,0:T(8,128)S(1)} custom-call(f32[1,1,128,128]{3,2,1,0:T(8,128)S(1)} %get-tuple-element.40), custom_call_target="InvertDiagBlocksLowerTriangular" | custom-call | tf_op jit(solution)/shard_map/jit(cholesky)/cholesky | solution.py:25
  168.7 11.7 %custom-call.74 = f32[1,128,128]{2,1,0:T(8,128)S(1)} custom-call(f32[1,128,128]{2,1,0:T(8,128)S(1)} %cholesky.586), custom_call_target="Cholesky" | custom-call | tf_op jit(solution)/shard_map/jit(cholesky)/cholesky | solution.py:25
  184.4 9.8 %custom-call.75 = f32[1,1,128,128]{2,3,1,0:T(8,128)S(1)} custom-call(f32[1,1,128,128]{3,2,1,0:T(8,128)S(1)} %get-tuple-element.38), custom_call_target="InvertDiagBlocksLowerTriangular" | custom-call | tf_op jit(solution)/shard_map/jit(cholesky)/cholesky | solution.py:25
  198.9 11.7 %custom-call.76 = f32[1,128,128]{2,1,0:T(8,128)S(1)} custom-call(f32[1,128,128]{2,1,0:T(8,128)S(1)} %cholesky.591), custom_call_target="Cholesky" | custom-call | tf_op jit(solution)/shard_map/jit(cholesky)/cholesky | solution.py:25
  211.3 9.8 %custom-call.77 = f32[1,1,128,128]{2,3,1,0:T(8,128)S(1)} custom-call(f32[1,1,128,128]{3,2,1,0:T(8,128)S(1)} %get-tuple-element.36), custom_call_target="InvertDiagBlocksLowerTriangular" | custom-call | tf_op jit(solution)/shard_map/jit(cholesky)/cholesky | solution.py:25
  225.7 11.7 %custom-call.78 = f32[1,128,128]{2,1,0:T(8,128)S(1)} custom-call(f32[1,128,128]{2,1,0:T(8,128)S(1)} %cholesky.596), custom_call_target="Cholesky" | custom-call | tf_op jit(solution)/shard_map/jit(cholesky)/cholesky | solution.py:25
  238.2 9.8 %custom-call.79 = f32[1,1,128,128]{2,3,1,0:T(8,128)S(1)} custom-call(f32[1,1,128,128]{3,2,1,0:T(8,128)S(1)} %get-tuple-element.34), custom_call_target="InvertDiagBlocksLowerTriangular" | custom-call | tf_op jit(solution)/shard_map/jit(cholesky)/cholesky | solution.py:25
  252.3 11.9 %custom-call.80 = f32[1,128,128]{2,1,0:T(8,128)S(1)} custom-call(f32[1,128,128]{2,1,0:T(8,128)S(1)} %cholesky.601), custom_call_target="Cholesky" | custom-call | tf_op jit(solution)/shard_map/jit(cholesky)/cholesky | solution.py:25
  265.0 9.8 %custom-call.81 = f32[1,1,128,128]{2,3,1,0:T(8,128)S(1)} custom-call(f32[1,1,128,128]{3,2,1,0:T(8,128)S(1)} %get-tuple-element.32), custom_call_target="InvertDiagBlocksLowerTriangular" | custom-call | tf_op jit(solution)/shard_map/jit(cholesky)/cholesky | solution.py:25
  279.0 11.7 %custom-call.82 = f32[1,128,128]{2,1,0:T(8,128)S(1)} custom-call(f32[1,128,128]{2,1,0:T(8,128)S(1)} %cholesky.606), custom_call_target="Cholesky" | custom-call | tf_op jit(solution)/shard_map/jit(cholesky)/cholesky | solution.py:25
  291.5 9.8 %custom-call.83 = f32[1,1,128,128]{2,3,1,0:T(8,128)S(1)} custom-call(f32[1,1,128,128]{3,2,1,0:T(8,128)S(1)} %get-tuple-element.30), custom_call_target="InvertDiagBlocksLowerTriangular" | custom-call | tf_op jit(solution)/shard_map/jit(cholesky)/cholesky | solution.py:25
  305.4 11.7 %custom-call.84 = f32[1,128,128]{2,1,0:T(8,128)S(1)} custom-call(f32[1,128,128]{2,1,0:T(8,128)S(1)} %cholesky.611), custom_call_target="Cholesky" | custom-call | tf_op jit(solution)/shard_map/jit(cholesky)/cholesky | solution.py:25
  317.9 9.8 %custom-call.85 = f32[1,1,128,128]{2,3,1,0:T(8,128)S(1)} custom-call(f32[1,1,128,128]{3,2,1,0:T(8,128)S(1)} %get-tuple-element.28), custom_call_target="InvertDiagBlocksLowerTriangular" | custom-call | tf_op jit(solution)/shard_map/jit(cholesky)/cholesky | solution.py:25
  330.7 11.7 %custom-call.86 = f32[1,128,128]{2,1,0:T(8,128)S(1)} custom-call(f32[1,128,128]{2,1,0:T(8,128)S(1)} %fusion.18), custom_call_target="Cholesky" | custom-call | tf_op jit(solution)/shard_map/jit(cholesky)/cholesky | solution.py:25
  352.9 4.9 select_select_fusion
  357.8 23.7 %while.1 = (s32[]{:T(128)}, f32[1,1024,1024]{1,2,0:T(8,128)}, s32[8,2]{0,1:T(2,128)S(1)}, f32[8,1,128,128]{3,2,1,0:T(8,128)S(1)}, s32[]{:T(128)}) while((s32[]{:T(128)}, f32[1,1024,1024]{1,2,0:T(8,128)}, s32[8,2]{0,1:T(2,128)S(1)}, f32[8,1,128,128]{3,2,1,0:T(8,128)S(1)}, s32[]{:T(128)}) %tuple.49), condition=%wide.while_cond, body=%wide.while_body.sunk | while | flops 2 | bytes 393333 | solution.py:8
  381.5 78.8 %custom-call.87 = f32[1,8,128,128]{2,3,1,0:T(8,128)S(1)} custom-call(f32[1,8,128,128]{3,2,1,0:T(8,128)S(1)} %bitcast.460), custom_call_target="InvertDiagBlocksLowerTriangular" | custom-call | tf_op jit(solution)/shard_map/triangular_solve | solution.py:8
  482.3 40.7 %all-gather.2.cloned.1.call-done = f32[1,512,1024]{2,1,0:T(8,128)} async-done(((f32[1,32,1024]{2,1,0:T(8,128)}), f32[1,512,1024]{2,1,0:T(8,128)}) %all-gather.2.cloned.1.call-update) | async-done | bytes 2097168 | tf_op jit(solution)/shard_map/all_gather | solution.py:31
  527.5 9.9 %reduce-scatter.2.cloned.1.call-done = f32[96,256]{1,0:T(8,128)} async-done(((f32[96,512]{1,0:T(8,128)}), f32[96,256]{1,0:T(8,128)}) %reduce-scatter.2.cloned.1.call-update) | async-done | bytes 98320 | tf_op jit(solution)/shard_map/reduce_scatter | solution.py:34
  (166 shorter events, 100.1 us)
Async XLA Ops:
  6.5 1.0 copy-start
  6.5 120.0 %all-reduce.3.cloned.1.call-start = ((), (), s32[]{:S(2)}) async-start(), calls=%async_computation.1 | async-start | bytes 8388608 | tf_op jit(solution)/shard_map/psum | solution.py:22
  12.6 510.4 %all-gather.2.cloned.1.call-start = ((), (), s32[]{:S(2)}) async-start(), calls=%async_computation.2 | async-start | bytes 2228224 | tf_op jit(solution)/shard_map/all_gather | solution.py:31
  141.8 1.9 copy-start.1
  352.9 107.4 %copy-start.3 = (f32[1,1,32,1024]{3,2,1,0:T(8,128)S(1)}, f32[1,1,32,1024]{3,2,1,0:T(8,128)}, u32[]{:S(2)}) copy-start(f32[1,1,32,1024]{3,2,1,0:T(8,128)} %param.4) | copy-start | bytes 393220
  481.6 0.7 copy-start.2
  482.3 55.1 %reduce-scatter.2.cloned.1.call-start = ((), (), s32[]{:S(2)}) async-start(), calls=%async_computation.3 | async-start | bytes 294912 | tf_op jit(solution)/shard_map/reduce_scatter | solution.py:34
Sparse Core Ops, SparseCore 0:
  12.7 113.8 all-reduce.2
  482.4 40.5 all-gather.1
  527.6 9.7 reduce-scatter.1
where the time goes:
time: 550 us; the launch traced here: 546 us
  other arithmetic  261 us (47%)
  waiting for transfers between devices  164 us (30%)
  matrix products  57.3 us (10%)
  local copies, waits for them, and re-layouts  43.8 us (8%)
  between operations  19.7 us (4%)
    another operation x30, other arithmetic, on_device(): factor = jnp.linalg.cholesky(fisher)  168 us
    psum x1, waiting for transfers between devices, on_device(): gram_matrix = lax.psum(partial_gram, ('ex', 'pb'))  113 us
    another operation x3, other arithmetic, solve_rows(): lax.linalg.triangular_solve(factor, rows_in, left_side=False, lower=True,...  83.6 us
    all_gather x1, waiting for transfers between devices, on_device(): lax.all_gather(solved, 'ex', axis=1, tiled=True)  40.7 us
    another operation x14, matrix products, on_device(): factor = jnp.linalg.cholesky(fisher)  27.2 us
    another operation x40, local copies, waits for them, and re-layouts  23.5 us
  transfers between devices with their start and end apart: 3, of which 3 were waited for; matrix products, arithmetic and copies ran while one was open for 0% of the time, Pallas kernels for 0%

commit v1 on v0

v1 whole, which is shorter than its diff:
```python
import functools
import jax
import jax.numpy as jnp
import numpy as np
from jax import lax
from jax.experimental import pallas as pl
from jax.experimental.pallas import tpu as pltpu
from jax.sharding import PartitionSpec as P

BLOCK = 128
SUB = 8
NT = (((1,), (1,)), ((), ()))
NN = (((1,), (0,)), ((), ()))
TN = (((0,), (0,)), ((), ()))
MESH = pl.DeviceIdType.MESH


def halves(x):
    hi = x.astype(jnp.bfloat16)
    return hi, (x - hi.astype(jnp.float32)).astype(jnp.bfloat16)


def dot3(a, b, dims):
    ah, al = a
    bh, bl = b
    dot = functools.partial(
        lax.dot_general, dimension_numbers=dims, preferred_element_type=jnp.float32
    )
    return dot(ah, bh) + (dot(ah, bl) + dot(al, bh))


def row_of(x, i):
    return jnp.broadcast_to(x[i : i + 1, :], x.shape)


def lane_of(x, i):
    return jnp.broadcast_to(x[:, i : i + 1], x.shape)


def invert_small(cols):
    sub = lax.broadcasted_iota(jnp.int32, cols[0].shape, 0)
    for j in range(SUB):
        inv = 1.0 / row_of(cols[j], j)
        here = sub == j
        pivot_col = cols[j]
        fresh = []
        for i in range(SUB):
            if i == j:
                fresh.append(jnp.where(here, inv, -pivot_col * inv))
            else:
                scaled = row_of(cols[i], j) * inv
                fresh.append(jnp.where(here, scaled, cols[i] - pivot_col * scaled))
        cols = fresh
    return cols


def invert_block(tiles, between):
    shape = tiles[0].shape
    sub = lax.broadcasted_iota(jnp.int32, shape, 0)
    lane = lax.broadcasted_iota(jnp.int32, shape, 1)
    count = len(tiles)
    for m in range(count):
        c0 = m * SUB
        inside = (lane >= c0) & (lane < c0 + SUB)
        panel = tiles[m]
        cols = invert_small([lane_of(panel, c0 + i) for i in range(SUB)])
        panel = jnp.where(inside, jnp.where(lane == sub + c0, 1.0, 0.0), panel)
        terms = [cols[i] * row_of(panel, i) for i in range(SUB)]
        solved = tree_sum(terms)
        rows = [row_of(solved, i) for i in range(SUB)]
        fresh = list(tiles)
        fresh[m] = solved
        order = [t % count for t in range(m + 1, m + count)]
        for t in order:
            tile = tiles[t]
            terms = [lane_of(tile, c0 + i) * rows[i] for i in range(SUB)]
            fresh[t] = jnp.where(inside, 0.0, tile) - tree_sum(terms)
        tiles = fresh
        between(m)
    return tiles


def tree_sum(terms):
    while len(terms) > 1:
        terms = [a + b for a, b in zip(terms[::2], terms[1::2])]
    return terms[0]


def pair(x):
    hi, lo = halves(x)
    return jnp.concatenate([hi, lo], axis=1)


def twice(x):
    hi, lo = halves(x)
    return jnp.concatenate([hi, hi], axis=1), jnp.concatenate([lo, lo], axis=1)


def dot4(a, b, dims):
    dot = functools.partial(
        lax.dot_general, dimension_numbers=dims, preferred_element_type=jnp.float32
    )
    return dot(a, b[0]) + dot(a, b[1])


def eliminate_kernel(inv_total, all_ref, damp_ref, x_ref, q_ref, out_ref,
                     z, diag, ch, cl, dh, dl, wx, xh, xl):
    n = all_ref.shape[1]
    nq, nx = q_ref.shape[0], x_ref.shape[0]
    cols = out_ref.shape[2]
    rows = z.shape[0]
    blocks = n // BLOCK
    chunks = BLOCK // SUB
    xh[...], xl[...] = halves(all_ref[...])
    wide = 2 * BLOCK
    for i in range(n // wide):
        at, upto = pl.ds(i * wide, wide), pl.ds(0, (i + 1) * wide)
        part = dot3((xh[:, at], xl[:, at]), (xh[:, upto], xl[:, upto]), TN)
        z[at, upto] = part * inv_total
    z[pl.ds(n, nq), :] = q_ref[...]
    z[pl.ds(n + nq, nx), :] = x_ref[...]
    damp = damp_ref[0]
    r = lax.broadcasted_iota(jnp.int32, (BLOCK, BLOCK), 0)
    c = lax.broadcasted_iota(jnp.int32, (BLOCK, BLOCK), 1)
    for b in range(blocks):
        at = pl.ds(b * BLOCK, BLOCK)
        z[at, at] = z[at, at] + jnp.where(r == c, damp, 0.0)
    for ref in (ch, cl, dh, dl, wx):
        ref[...] = jnp.zeros_like(ref)
    out_ref[...] = jnp.zeros_like(out_ref)
    diag[...] = z[pl.ds(0, BLOCK), pl.ds(0, BLOCK)]

    def solve_rows(at, column):
        c_rows = z[at, column]
        w = pair(dot4(pair(c_rows), (dh[...], dl[...]), NT))
        if at.start >= n and at.start < n + nq:
            ch[at, :], cl[at, :] = twice(c_rows)
        if at.start + at.size > n + nq:
            skip = max(n + nq - at.start, 0)
            wx[pl.ds(at.start + skip - n - nq, at.size - skip), :] = w[skip:]
        return w

    def add_scores():
        for j in range(out_ref.shape[0]):
            qs = pl.ds(n + j * cols, cols)
            out_ref[j] += dot4(wx[...], (ch[qs, :], cl[qs, :]), NT)

    def segment(first, last):
        row_lo, col_lo = (first + 1) * BLOCK, first * BLOCK
        step = -(-(rows - row_lo) // (chunks * 16)) * 16
        if (n - row_lo) % step:
            cuts = list(range(row_lo, n, step)) + list(range(n, rows, step)) + [rows]
        else:
            cuts = list(range(row_lo, rows, step)) + [rows]
        spans = [pl.ds(lo, hi - lo) for lo, hi in zip(cuts, cuts[1:])]
        right = pl.ds(col_lo, n - col_lo)

        def body(k, carry):
            column = pl.ds(pl.multiple_of(jnp.maximum(k - 1, 0) * BLOCK, BLOCK), BLOCK)

            def bulk(m):
                mine = spans[m * len(spans) // chunks : (m + 1) * len(spans) // chunks]
                for at in mine:
                    w = solve_rows(at, column)
                    z[at, right] = z[at, right] - dot4(w, (ch[right, :], cl[right, :]), NT)
                if m == chunks - 1:
                    add_scores()

            tiles = [diag[pl.ds(t * SUB, SUB), :] for t in range(chunks)]
            tiles = invert_block(tiles, bulk)
            inverse = jnp.concatenate(tiles, axis=0)
            dh[...], dl[...] = twice(inverse)
            base = pl.multiple_of(k * BLOCK, BLOCK)
            panel = z[right, pl.ds(base, BLOCK)]
            row_at = col_lo + lax.broadcasted_iota(jnp.int32, panel.shape, 0)
            ch[right, :], cl[right, :] = twice(jnp.where(row_at >= base + BLOCK, panel, 0.0))
            nxt = pl.multiple_of(jnp.minimum(k + 1, blocks - 1) * BLOCK, BLOCK)
            at = pl.ds(nxt, BLOCK)
            c_next = z[at, pl.ds(base, BLOCK)]
            w_next = pair(dot4(pair(c_next), twice(inverse), NT))
            diag[...] = z[at, at] - dot4(w_next, twice(c_next), NT)
            return carry

        lax.fori_loop(first, last, body, 0)

    for first in range(0, blocks, 2):
        segment(first, min(first + 2, blocks))
    ends = pl.ds((blocks - 1) * BLOCK, BLOCK)
    solve_rows(pl.ds(n, nq), ends)
    solve_rows(pl.ds(n + nq, nx), ends)
    add_scores()


def eliminate(x_all, damping, x, q, parts):
    total, n = x_all.shape
    rows = n + x.shape[0] + q.shape[0]
    vmem = pl.BlockSpec(memory_space=pltpu.VMEM)
    return pl.pallas_call(
        functools.partial(eliminate_kernel, 1.0 / total),
        out_shape=jax.ShapeDtypeStruct(
            (parts, x.shape[0], q.shape[0] // parts), jnp.float32
        ),
        in_specs=[vmem, pl.BlockSpec(memory_space=pltpu.SMEM), vmem, vmem],
        out_specs=vmem,
        scratch_shapes=[
            pltpu.VMEM((rows, n), jnp.float32),
            pltpu.VMEM((BLOCK, BLOCK), jnp.float32),
            pltpu.VMEM((rows, 2 * BLOCK), jnp.bfloat16),
            pltpu.VMEM((rows, 2 * BLOCK), jnp.bfloat16),
            pltpu.VMEM((BLOCK, 2 * BLOCK), jnp.bfloat16),
            pltpu.VMEM((BLOCK, 2 * BLOCK), jnp.bfloat16),
            pltpu.VMEM((x.shape[0], 2 * BLOCK), jnp.bfloat16),
            pltpu.VMEM((total, n), jnp.bfloat16),
            pltpu.VMEM((total, n), jnp.bfloat16),
        ],
        compiler_params=pltpu.CompilerParams(vmem_limit_bytes=60 * 1024 * 1024),
    )(x_all, damping, x, q)


UP, DOWN, SIDE, CORE = range(4)


def gather_kernel(dims, x_ref, q_ref, x_all, q_all, x_send, x_recv, q_send, q_recv, own_sem):
    line, across, cores = dims
    me = lax.axis_index("ex")
    core = lax.rem(me, cores)
    side = lax.rem(me // cores, across)
    at = me // (cores * across)

    def index(z, y, c):
        return (z * across + y) * cores + c

    has_up, has_down = at < line - 1, at > 0
    targets = {
        UP: index(jnp.minimum(at + 1, line - 1), side, core),
        DOWN: index(jnp.maximum(at - 1, 0), side, core),
        SIDE: index(at, across - 1 - side, core),
        CORE: index(at, side, cores - 1 - core),
    }
    exists = {UP: has_up, DOWN: has_down, SIDE: True, CORE: True}
    kinds = [k for k, on in ((UP, line > 1), (DOWN, line > 1), (SIDE, across > 1), (CORE, cores > 1)) if on]

    def guarded(cond, fn):
        if cond is True:
            fn()
        else:
            pl.when(cond)(fn)

    def both(a, b):
        if a is True:
            return b
        return a if b is True else a & b

    barrier = pltpu.get_barrier_semaphore()
    for kind in kinds:
        def hello(kind=kind):
            pl.semaphore_signal(barrier, inc=1, device_id={"ex": targets[kind]}, device_id_type=MESH)
        guarded(exists[kind], hello)
    peers = sum(1 if exists[k] is True else exists[k].astype(jnp.int32) for k in kinds)
    pl.semaphore_wait(barrier, peers)

    arrays = {"x": (x_ref, x_all, x_send, x_recv), "q": (q_ref, q_all, q_send, q_recv)}
    sent = []

    def copy(name, block, kind, own):
        ref, whole, send, recv = arrays[name]
        height = ref.shape[0]
        rows = whole.at[pl.ds(pl.multiple_of(block * height, 8), height), :]
        return pltpu.make_async_remote_copy(
            src_ref=ref if own else rows, dst_ref=rows,
            send_sem=send.at[block, kind], recv_sem=recv.at[block],
            device_id={"ex": targets[kind]}, device_id_type=MESH,
        )

    def push(name, block, wanted, valid=True, own=False):
        for kind in wanted:
            if kind in kinds:
                cond = both(valid, exists[kind])
                guarded(cond, lambda kind=kind: copy(name, block, kind, own).start())
                sent.append((name, block, kind, own, cond))

    def landed(name, block, valid=True):
        guarded(valid, lambda: copy(name, block, CORE, False).wait_recv())

    def relay(name, block, wanted, valid=True):
        landed(name, block, valid)
        push(name, block, wanted, valid)

    push("x", me, (UP, DOWN, SIDE, CORE), own=True)
    push("q", me, (SIDE, UP, DOWN, CORE), own=True)
    own_copies = []
    for slot, name in enumerate(arrays):
        ref, whole, _, _ = arrays[name]
        height = ref.shape[0]
        own_copies.append(pltpu.make_async_copy(
            ref, whole.at[pl.ds(pl.multiple_of(me * height, 8), height), :], own_sem.at[slot]
        ))
        own_copies[-1].start()
    other = across - 1 - side

    def crossed(s):
        for z, valid in spots(s):
            relay("x", index(z, other, core), (CORE,), valid)

    def spots(s):
        if s == 0:
            return [(at, True)]
        return [
            (jnp.maximum(at - s, 0), at - s >= 0),
            (jnp.minimum(at + s, line - 1), at + s <= line - 1),
        ]

    if across > 1:
        relay("q", index(at, other, core), (UP, DOWN, CORE))
    for s in range(1, line):
        for (z, valid), onward in zip(spots(s), (UP, DOWN)):
            relay("x", index(z, side, core), (onward, SIDE, CORE), valid)
        for (z, valid), onward in zip(spots(s), (UP, DOWN)):
            relay("q", index(z, side, core), (onward, CORE), valid)
            if across > 1:
                relay("q", index(z, other, core), (onward, CORE), valid)
        if across > 1:
            crossed(s - 1)
    if across > 1:
        crossed(line - 1)
    if cores > 1:
        for z in range(line):
            for y in range(across):
                for name in arrays:
                    landed(name, index(z, y, cores - 1 - core))
    for c in own_copies:
        c.wait()
    for name, block, kind, own, cond in sent:
        guarded(cond, lambda: copy(name, block, kind, own).wait_send())


def gather(x, q, dims):
    count = dims[0] * dims[1] * dims[2]
    vmem = pl.BlockSpec(memory_space=pltpu.VMEM)
    hbm = pl.BlockSpec(memory_space=pl.ANY)
    dma = pltpu.SemaphoreType.DMA
    return pl.pallas_call(
        functools.partial(gather_kernel, dims),
        out_shape=[
            jax.ShapeDtypeStruct((count * a.shape[0], a.shape[1]), a.dtype) for a in (x, q)
        ],
        in_specs=[vmem, vmem],
        out_specs=[hbm, hbm],
        scratch_shapes=[dma((count, 4)), dma((count,)), dma((count, 4)), dma((count,)), dma((2,))],
        compiler_params=pltpu.CompilerParams(collective_id=0, has_side_effects=True),
    )(x, q)


def swap_kernel(layers, score_ref, got_ref, send, recv, own_sem):
    me = lax.axis_index("layer")
    barrier = pltpu.get_barrier_semaphore()
    copies = []
    for d in range(1, layers):
        peer = lax.rem(me + d, layers)
        pl.semaphore_signal(barrier, inc=1, device_id={"layer": peer}, device_id_type=MESH)
    own = pltpu.make_async_copy(score_ref.at[me], got_ref.at[me], own_sem)
    own.start()
    pl.semaphore_wait(barrier, layers - 1)
    for d in range(1, layers):
        peer = lax.rem(me + d, layers)
        copies.append(pltpu.make_async_remote_copy(
            src_ref=score_ref.at[peer], dst_ref=got_ref.at[me],
            send_sem=send.at[d], recv_sem=recv.at[d],
            device_id={"layer": peer}, device_id_type=MESH,
        ))
        copies[-1].start()
    for d, c in enumerate(copies, 1):
        c.wait_send()
        source = lax.rem(me + layers - d, layers)
        pltpu.make_async_remote_copy(
            src_ref=score_ref.at[source], dst_ref=got_ref.at[source],
            send_sem=send.at[d], recv_sem=recv.at[d],
            device_id={"layer": source}, device_id_type=MESH,
        ).wait_recv()
    own.wait()


def swap(score):
    layers = score.shape[0]
    if layers == 1:
        return score[0]
    vmem = pl.BlockSpec(memory_space=pltpu.VMEM)
    dma = pltpu.SemaphoreType.DMA
    got = pl.pallas_call(
        functools.partial(swap_kernel, layers),
        out_shape=jax.ShapeDtypeStruct(score.shape, score.dtype),
        in_specs=[vmem],
        out_specs=vmem,
        scratch_shapes=[dma((layers,)), dma((layers,)), dma],
        compiler_params=pltpu.CompilerParams(collective_id=1, has_side_effects=True),
    )(score)
    return jnp.sum(got, axis=0)


def line_dims(mesh):
    axis = mesh.axis_names.index("ex")
    devices = np.moveaxis(mesh.devices, axis, 0).reshape(mesh.shape["ex"], -1)[:, 0]
    count = len(devices)
    places = [tuple(getattr(d, "coords", None) or (i,)) for i, d in enumerate(devices)]
    cores = 2 if count % 2 == 0 and places[0] == places[1] else 1
    chips = places[::cores]
    if len(chips) % 2 or len(chips) < 4:
        return count // cores, 1, cores
    step = [a != b for a, b in zip(chips[0], chips[1])]
    back = [a != b for a, b in zip(chips[0], chips[2])]
    across = 2 if step != back else 1
    return len(chips) // across, across, cores


def solution(mesh):
    dims = line_dims(mesh)

    def on_device(train_grads, query_grads, damping):
        layers_here = train_grads.shape[0]
        parts = lax.axis_size("layer")
        score = None
        for l in range(layers_here):
            x, q = train_grads[l], query_grads[l, 0]
            x_all, q_all = gather(x, q, dims)
            term = eliminate(x_all, damping[l : l + 1], x, q_all, parts)
            score = term if score is None else score + term
        return swap(score)[:, None, :]

    in_specs = (
        P("layer", ("groups", "ex"), None),
        P("layer", "pb", ("groups", "ex"), None),
        P("layer"),
    )
    out_specs = P(("groups", "ex"), "pb", "layer")
    return jax.shard_map(
        on_device, mesh=mesh, in_specs=in_specs, out_specs=out_specs, check_vma=False
    )
```

time: 550 us -> 142 us (0.26)
  other arithmetic: 261 us -> 0.95 us
  waiting for transfers between devices: 164 us -> 0 us
  Pallas kernels: 0 us -> 139 us
  matrix products: 57.3 us -> 0 us
  local copies, waits for them, and re-layouts: 43.8 us -> 0.71 us
  between operations: 19.7 us -> 0.67 us
    another operation x33 -> x0, other arithmetic: 251 us -> none  [the longest x30 168 us: on_device(): factor = jnp.linalg.cholesky(fisher)]
    pallas_call x0 -> x3, Pallas kernels: none -> 139 us  [the longest x1 76.4 us: eliminate(): pl.pallas_call(functools.partial(eliminate_kernel, 1.0 / total), out_shap...]
    psum x1 -> x0, waiting for transfers between devices: 113 us -> none  [on_device(): gram_matrix = lax.psum(partial_gram, ('ex', 'pb'))]
    another operation x44 -> x0, matrix products: 47.8 us -> none  [the longest x14 27.2 us: on_device(): factor = jnp.linalg.cholesky(fisher)]
    all_gather x1 -> x0, waiting for transfers between devices: 40.7 us -> none  [on_device(): lax.all_gather(solved, 'ex', axis=1, tiled=True)]
    another operation x70 -> x0, local copies, waits for them, and re-layouts: 32.8 us -> none
    reduce_scatter x1 -> x0, waiting for transfers between devices: 9.91 us -> none  [on_device(): lax.psum_scatter(score_tile, 'layer', scatter_dimension=1, tiled=True)]
    dot_general x2 -> x0, matrix products: 9.46 us -> none  [the longest x1 5.03 us: on_device(): jnp.einsum('lnp,lnq->lpq', own_rows, own_rows, precision=lax.Precision.HI...]
  transfers between devices with their start and end apart: 3 -> 0, of which waited for: 3 -> 0; matrix products, arithmetic and copies ran while one was open for 0% -> 0% of each run, Pallas kernels for 0% -> 0%
where the time goes in v1:
time: 142 us
  Pallas kernels  139 us (98%)
    pallas_call x1, Pallas kernels, eliminate(): pl.pallas_call(functools.partial(eliminate_kernel, 1.0 / total), out_shap...  76.4 us
    pallas_call x1, Pallas kernels, gather(): pl.pallas_call(functools.partial(gather_kernel, dims), out_shape=[jax.Sha...  56 us
    pallas_call x1, Pallas kernels, swap(): pl.pallas_call(functools.partial(swap_kernel, layers), out_shape=jax.Shap...  6.77 us

profile of v1, /device:TPU:0, one launch (start us, length us, event | category | flops | bytes accessed | tf_op | source)
XLA Modules:
  0.0 141.5 jit_solution(5971308908019697958)
XLA Ops:
  0.7 56.0 %shard_map.37 = (f32[1536,1024]{1,0:T(8,128)}, f32[512,1024]{1,0:T(8,128)}) custom-call(f32[96,1024]{1,0:T(8,128)} %bitcast.2, f32[32,1024]{1,0:T(8,128)} %bitcast.4), custom_call_target="tpu_custom_call" | custom-call | tf_op jit(solution)/shard_map/pallas_call | solution.py:342
  56.7 76.4 %shard_map.38.score_ref = f32[2,96,256]{2,1,0:T(8,128)} custom-call(f32[1536,1024]{1,0:T(8,128)} %get-tuple-element.7.all_ref, f32[1]{0:T(128)S(6)} %copy.4.damp_ref, f32[96,1024]{1,0:T(8,128)} %bitcast.3, f32[512,1024]{1,0:T(8,128)} %get-tuple-element.8.q_ref), custom_call_target="tpu_custom_call" | custom-call | tf_op jit(solution)/shard_map/pallas_call | solution.py:198
  133.1 6.8 %shard_map.39 = f32[2,96,256]{2,1,0:T(8,128)} custom-call(f32[2,96,256]{2,1,0:T(8,128)} %shard_map.38.score_ref), custom_call_target="tpu_custom_call" | custom-call | tf_op jit(solution)/shard_map/pallas_call | solution.py:389
  139.9 1.0 reduce_sum.9
  140.8 0.7 broadcast_in_dim.3

commit v2 on v1

--- a/solution.py
+++ b/solution.py
@@ -27,6 +27,23 @@
         lax.dot_general, dimension_numbers=dims, preferred_element_type=jnp.float32
     )
     return dot(ah, bh) + (dot(ah, bl) + dot(al, bh))
+
+
+def pair(x):
+    hi, lo = halves(x)
+    return jnp.concatenate([hi, lo], axis=1)
+
+
+def twice(x):
+    hi, lo = halves(x)
+    return jnp.concatenate([hi, hi], axis=1), jnp.concatenate([lo, lo], axis=1)
+
+
+def dot4(a, b, dims):
+    dot = functools.partial(
+        lax.dot_general, dimension_numbers=dims, preferred_element_type=jnp.float32
+    )
+    return dot(a, b[0]) + dot(a, b[1])
 
 
 def row_of(x, i):
@@ -86,31 +103,15 @@
     return terms[0]
 
 
-def pair(x):
-    hi, lo = halves(x)
-    return jnp.concatenate([hi, lo], axis=1)
-
-
-def twice(x):
-    hi, lo = halves(x)
-    return jnp.concatenate([hi, hi], axis=1), jnp.concatenate([lo, lo], axis=1)
-
-
-def dot4(a, b, dims):
-    dot = functools.partial(
-        lax.dot_general, dimension_numbers=dims, preferred_element_type=jnp.float32
-    )
-    return dot(a, b[0]) + dot(a, b[1])
-
-
 def eliminate_kernel(inv_total, all_ref, damp_ref, x_ref, q_ref, out_ref,
-                     z, diag, ch, cl, dh, dl, wx, xh, xl):
+                     z, diag, wp, ch, cl, xh, xl):
     n = all_ref.shape[1]
     nq, nx = q_ref.shape[0], x_ref.shape[0]
     cols = out_ref.shape[2]
     rows = z.shape[0]
     blocks = n // BLOCK
     chunks = BLOCK // SUB
+    step = rows // chunks
     xh[...], xl[...] = halves(all_ref[...])
     wide = 2 * BLOCK
     for i in range(n // wide):
@@ -119,81 +120,64 @@
         z[at, upto] = part * inv_total
     z[pl.ds(n, nq), :] = q_ref[...]
     z[pl.ds(n + nq, nx), :] = x_ref[...]
+    if rows > n + nq + nx:
+        z[pl.ds(n + nq + nx, rows - n - nq - nx), :] = jnp.zeros(
+            (rows - n - nq - nx, n), jnp.float32
+        )
     damp = damp_ref[0]
     r = lax.broadcasted_iota(jnp.int32, (BLOCK, BLOCK), 0)
     c = lax.broadcasted_iota(jnp.int32, (BLOCK, BLOCK), 1)
     for b in range(blocks):
         at = pl.ds(b * BLOCK, BLOCK)
         z[at, at] = z[at, at] + jnp.where(r == c, damp, 0.0)
-    for ref in (ch, cl, dh, dl, wx):
+    for ref in (wp, ch, cl):
         ref[...] = jnp.zeros_like(ref)
     out_ref[...] = jnp.zeros_like(out_ref)
     diag[...] = z[pl.ds(0, BLOCK), pl.ds(0, BLOCK)]
 
-    def solve_rows(at, column):
-        c_rows = z[at, column]
-        w = pair(dot4(pair(c_rows), (dh[...], dl[...]), NT))
-        if at.start >= n and at.start < n + nq:
-            ch[at, :], cl[at, :] = twice(c_rows)
-        if at.start + at.size > n + nq:
-            skip = max(n + nq - at.start, 0)
-            wx[pl.ds(at.start + skip - n - nq, at.size - skip), :] = w[skip:]
-        return w
-
-    def add_scores():
-        for j in range(out_ref.shape[0]):
-            qs = pl.ds(n + j * cols, cols)
-            out_ref[j] += dot4(wx[...], (ch[qs, :], cl[qs, :]), NT)
-
     def segment(first, last):
         row_lo, col_lo = (first + 1) * BLOCK, first * BLOCK
-        step = -(-(rows - row_lo) // (chunks * 16)) * 16
-        if (n - row_lo) % step:
-            cuts = list(range(row_lo, n, step)) + list(range(n, rows, step)) + [rows]
-        else:
-            cuts = list(range(row_lo, rows, step)) + [rows]
-        spans = [pl.ds(lo, hi - lo) for lo, hi in zip(cuts, cuts[1:])]
-        right = pl.ds(col_lo, n - col_lo)
+        step = (rows - row_lo) // chunks
+        right, below = pl.ds(col_lo, n - col_lo), pl.ds(row_lo, rows - row_lo)
 
         def body(k, carry):
-            column = pl.ds(pl.multiple_of(jnp.maximum(k - 1, 0) * BLOCK, BLOCK), BLOCK)
-
             def bulk(m):
-                mine = spans[m * len(spans) // chunks : (m + 1) * len(spans) // chunks]
-                for at in mine:
-                    w = solve_rows(at, column)
-                    z[at, right] = z[at, right] - dot4(w, (ch[right, :], cl[right, :]), NT)
-                if m == chunks - 1:
-                    add_scores()
+                at = pl.ds(row_lo + m * step, step)
+                z[at, right] = z[at, right] - dot4(wp[at, :], (ch[right, :], cl[right, :]), NT)
 
             tiles = [diag[pl.ds(t * SUB, SUB), :] for t in range(chunks)]
             tiles = invert_block(tiles, bulk)
-            inverse = jnp.concatenate(tiles, axis=0)
-            dh[...], dl[...] = twice(inverse)
+            inverse = twice(jnp.concatenate(tiles, axis=0))
             base = pl.multiple_of(k * BLOCK, BLOCK)
-            panel = z[right, pl.ds(base, BLOCK)]
-            row_at = col_lo + lax.broadcasted_iota(jnp.int32, panel.shape, 0)
-            ch[right, :], cl[right, :] = twice(jnp.where(row_at >= base + BLOCK, panel, 0.0))
+            panel = z[below, pl.ds(base, BLOCK)]
+            row_at = row_lo + lax.broadcasted_iota(jnp.int32, panel.shape, 0)
+            panel = jnp.where(row_at >= base + BLOCK, panel, 0.0)
+            if first:
+                ch[pl.ds(col_lo, BLOCK), :] = jnp.zeros((BLOCK, 2 * BLOCK), jnp.bfloat16)
+                cl[pl.ds(col_lo, BLOCK), :] = jnp.zeros((BLOCK, 2 * BLOCK), jnp.bfloat16)
+            hi, lo = halves(panel)
+            ch[below, :] = jnp.concatenate([hi, hi], axis=1)
+            cl[below, :] = jnp.concatenate([lo, lo], axis=1)
+            wp[below, :] = pair(dot4(jnp.concatenate([hi, lo], axis=1), inverse, NT))
             nxt = pl.multiple_of(jnp.minimum(k + 1, blocks - 1) * BLOCK, BLOCK)
             at = pl.ds(nxt, BLOCK)
-            c_next = z[at, pl.ds(base, BLOCK)]
-            w_next = pair(dot4(pair(c_next), twice(inverse), NT))
-            diag[...] = z[at, at] - dot4(w_next, twice(c_next), NT)
+            diag[...] = z[at, at] - dot4(wp[at, :], (ch[at, :], cl[at, :]), NT)
+            xs = pl.ds(n + nq, nx)
+            for j in range(out_ref.shape[0]):
+                qs = pl.ds(n + j * cols, cols)
+                out_ref[j] += dot4(wp[xs, :], (ch[qs, :], cl[qs, :]), NT)
             return carry
 
         lax.fori_loop(first, last, body, 0)
 
-    for first in range(0, blocks, 2):
-        segment(first, min(first + 2, blocks))
-    ends = pl.ds((blocks - 1) * BLOCK, BLOCK)
-    solve_rows(pl.ds(n, nq), ends)
-    solve_rows(pl.ds(n + nq, nx), ends)
-    add_scores()
+    half = blocks // 2
+    segment(0, half)
+    segment(half, blocks)
 
 
 def eliminate(x_all, damping, x, q, parts):
     total, n = x_all.shape
-    rows = n + x.shape[0] + q.shape[0]
+    rows = -(-(n + x.shape[0] + q.shape[0]) // 256) * 256
     vmem = pl.BlockSpec(memory_space=pltpu.VMEM)
     return pl.pallas_call(
         functools.partial(eliminate_kernel, 1.0 / total),
@@ -207,9 +191,7 @@
             pltpu.VMEM((BLOCK, BLOCK), jnp.float32),
             pltpu.VMEM((rows, 2 * BLOCK), jnp.bfloat16),
             pltpu.VMEM((rows, 2 * BLOCK), jnp.bfloat16),
-            pltpu.VMEM((BLOCK, 2 * BLOCK), jnp.bfloat16),
-            pltpu.VMEM((BLOCK, 2 * BLOCK), jnp.bfloat16),
-            pltpu.VMEM((x.shape[0], 2 * BLOCK), jnp.bfloat16),
+            pltpu.VMEM((rows, 2 * BLOCK), jnp.bfloat16),
             pltpu.VMEM((total, n), jnp.bfloat16),
             pltpu.VMEM((total, n), jnp.bfloat16),
         ],

time: 142 us -> 129 us (0.908)
  Pallas kernels: 139 us -> 126 us
    pallas_call x1, Pallas kernels: 76.4 us -> 63.4 us  [eliminate(): pl.pallas_call(functools.partial(eliminate_kernel, 1.0 / total), out_shap...]
where the time goes in v2:
time: 129 us; the launch traced here: 128 us
  Pallas kernels  126 us (98%)
    pallas_call x1, Pallas kernels, eliminate(): pl.pallas_call(functools.partial(eliminate_kernel, 1.0 / total), out_shap...  63.4 us
    pallas_call x1, Pallas kernels, gather(): pl.pallas_call(functools.partial(gather_kernel, dims), out_shape=[jax.Sha...  56 us
    pallas_call x1, Pallas kernels, swap(): pl.pallas_call(functools.partial(swap_kernel, layers), out_shape=jax.Shap...  6.77 us

profile of v2, /device:TPU:0, one launch (start us, length us, event | category | flops | bytes accessed | tf_op | source)
XLA Modules:
  0.0 128.5 jit_solution(5182495402576818761)
XLA Ops:
  0.7 56.0 %shard_map.37 = (f32[1536,1024]{1,0:T(8,128)}, f32[512,1024]{1,0:T(8,128)}) custom-call(f32[96,1024]{1,0:T(8,128)} %bitcast.2, f32[32,1024]{1,0:T(8,128)} %bitcast.4), custom_call_target="tpu_custom_call" | custom-call | tf_op jit(solution)/shard_map/pallas_call | solution.py:324
  56.7 63.4 %shard_map.38.score_ref = f32[2,96,256]{2,1,0:T(8,128)} custom-call(f32[1536,1024]{1,0:T(8,128)} %get-tuple-element.7.all_ref, f32[1]{0:T(128)S(6)} %copy.4.damp_ref, f32[96,1024]{1,0:T(8,128)} %bitcast.3, f32[512,1024]{1,0:T(8,128)} %get-tuple-element.8.q_ref), custom_call_target="tpu_custom_call" | custom-call | tf_op jit(solution)/shard_map/pallas_call | solution.py:182
  120.1 6.8 %shard_map.39 = f32[2,96,256]{2,1,0:T(8,128)} custom-call(f32[2,96,256]{2,1,0:T(8,128)} %shard_map.38.score_ref), custom_call_target="tpu_custom_call" | custom-call | tf_op jit(solution)/shard_map/pallas_call | solution.py:371
  126.8 1.0 reduce_sum.9
  127.8 0.7 broadcast_in_dim.3
